TPU v7x, 256 devices: a whole 4x4x8 slice. The times are simulated.
256 devices in a mesh: store: 16 (over y, x_hi, core), dept: 16 (over z, x_lo).
Axes of the slice: x: 4 (x_hi: 2, x_lo: 2; x = x_hi * 2 + x_lo), y: 4, z: 8, core: 2. Of those that a mesh axis runs over, the one named last changes fastest.
Arguments:
- history: bfloat16 [4096, 384, 512], P('store', 'dept'), may hold values from -400 to 400, as said below
- input_layer_matrix: bfloat16 [512, 512], replicated, may hold values from -0.375 to 0.375
- middle_layer_matrix: bfloat16 [512, 512], replicated, may hold values from -0.375 to 0.375
- final_layer_matrix: bfloat16 [512, 28], replicated, may hold values from -0.375 to 0.375
Outputs:
- reconciled: float32 [4096, 10752], P('store', 'dept')
- store_gap: float32 [28, 4096], P(None, 'store')
- item_gap: float32 [28, 384], P(None, 'dept')
Inputs may be any that keep to these rules, and one draw needn't show every extreme that they name: `history`: daily sales histories.
All inputs are finite; a program needn't handle non-finite values.
Results may differ from a plain program's by a relative error of at most 0.0065.
The roundings to bfloat16 on the way count: a program that leaves them out, or rounds other values in their place, can miss the bound.
Values sent between devices are 32-bit elements; how exact they have to be, the bound alone decides.
No kernel may reach another device: no remote copies, remote signals or barrier semaphores. Data moves between devices by JAX's collectives and lax.ppermute only.
A program may use at most 64 MiB of HBM per device.

v0:
```python
import math
import jax
import jax.numpy as jnp
from jax import lax
from jax.sharding import PartitionSpec as P


def predictor_function(sequence_grid, input_layer_matrix, middle_layer_matrix, final_layer_matrix):
    values = sequence_grid.astype(jnp.float32)
    root_mean = jnp.sqrt(jnp.mean(values * values, axis=-1, keepdims=True) + 1e-05)
    scaled = (values / root_mean).astype(jnp.bfloat16)
    hidden_one = jax.nn.relu(
        jnp.dot(scaled, input_layer_matrix, preferred_element_type=jnp.float32)
    ).astype(jnp.bfloat16)
    hidden_two = jax.nn.relu(
        jnp.dot(hidden_one, middle_layer_matrix, preferred_element_type=jnp.float32)
    ).astype(jnp.bfloat16)
    return jnp.dot(hidden_two, final_layer_matrix, preferred_element_type=jnp.float32) * root_mean


def body(history, input_layer_matrix, middle_layer_matrix, final_layer_matrix):
    store_row_set, item_columns, history_count = history.shape
    horizon = final_layer_matrix.shape[1]
    widened_entries = history.astype(jnp.float32)
    store_part = jnp.sum(widened_entries, axis=1)
    item_part = jnp.sum(widened_entries, axis=0)
    product_past_sales = lax.psum(item_part, "store")
    outlet_past_sales = lax.psum(store_part, "dept")
    outlet_estimate = predictor_function(
        outlet_past_sales, input_layer_matrix, middle_layer_matrix, final_layer_matrix
    )
    product_estimate = predictor_function(
        product_past_sales, input_layer_matrix, middle_layer_matrix, final_layer_matrix
    )
    finest_tier = predictor_function(
        history.reshape(store_row_set * item_columns, history_count),
        input_layer_matrix,
        middle_layer_matrix,
        final_layer_matrix,
    )
    finest_tier = finest_tier.reshape(store_row_set, item_columns, horizon)
    row_part = jnp.sum(finest_tier, axis=1)
    col_part = jnp.sum(finest_tier, axis=0)
    row_sum = lax.psum(row_part, "dept")
    col_sum = lax.psum(col_part, "store")
    store_err = outlet_estimate - row_sum
    item_err = product_estimate - col_sum
    err_s = lax.psum(jnp.sum(store_err, axis=0), "store")
    err_i = lax.psum(jnp.sum(item_err, axis=0), "dept")
    item_count = float(item_columns * lax.axis_size("dept"))
    store_count = float(store_row_set * lax.axis_size("store"))
    denominator = 1.0 + item_count + store_count
    shift_s = (err_s * (1.0 + store_count) - store_count * err_i) / denominator
    shift_i = ((1.0 + item_count) * err_i - item_count * err_s) / denominator
    store_shift = (store_err - shift_i) / (1.0 + item_count)
    item_shift = (item_err - shift_s) / (1.0 + store_count)
    reconciled = finest_tier + store_shift[:, None, :] + item_shift[None, :, :]
    store_gap = (store_err / math.sqrt(item_count)).T
    item_gap = (item_err / math.sqrt(store_count)).T
    return (reconciled.reshape(store_row_set, item_columns * horizon), store_gap, item_gap)


def solution(mesh):
    return jax.shard_map(
        body,
        mesh=mesh,
        in_specs=(P("store", "dept", None), P(), P(), P()),
        out_specs=(P("store", "dept"), P(None, "store"), P(None, "dept")),
        check_vma=False,
    )
```

profile of v0, /device:TPU:1, one launch (start us, length us, event | category | flops | bytes accessed | tf_op | source)
XLA Modules:
  0.0 231.8 jit_solution(3153932601823036586)
XLA Ops:
  7.2 0.0 copy-start
  7.2 0.0 all-reduce.4.cloned.1.call-start
  7.2 6.6 %convert_reduce_fusion = (f32[24,512]{1,0:T(8,128)S(1)}, f32[256,24]{1,0:T(8,128)S(1)}, f32[256,512]{1,0:T(8,128)}) fusion(bf16[256,24,512]{2,1,0:T(8,128)(2,1)} %param.4), kind=kLoop, calls=%fused_computation.5 | loop fusion | flops 15579136 | bytes 6889472 | tf_op jit(solution)/shard_map/reduce_sum | solution.py:26
  13.8 0.0 all-reduce.4.cloned.1.call-update
  13.9 0.1 sqrt.28
  14.0 0.0 copy-start.1
  14.0 7.2 %fusion = bf16[6144,512]{1,0:T(8,128)(2,1)} fusion(bf16[256,24,512]{2,1,0:T(8,128)(2,1)} %param.4, f32[6144]{0:T(1024)S(1)} %sqrt.28), kind=kLoop, calls=%fused_computation.1 | loop fusion | flops 9437184 | bytes 12607488 | tf_op jit(solution)/shard_map/convert_element_type | solution.py:11
  21.3 0.0 copy-done
  21.3 10.4 %maximum_convert_fusion = bf16[6144,512]{1,0:T(8,128)(2,1)} fusion(bf16[512,512]{1,0:T(8,128)(2,1)S(1)} %copy-done, bf16[6144,512]{1,0:T(8,128)(2,1)} %fusion, bf16[512,512]{1,0:T(8,128)(2,1)S(1)} %copy-done.1), kind=kOutput, calls=%fused_computation.2 | convolution fusion | flops 6455033856 | bytes 13631488 | tf_op jit(solution)/shard_map/dot_general | solution.py:16
  31.7 4.7 %convolution_multiply_fusion = f32[6144,28]{0,1:T(8,128)S(1)} fusion(bf16[6144,512]{1,0:T(8,128)(2,1)} %maximum_convert_fusion, bf16[512,28]{0,1:T(8,128)(2,1)S(1)} %copy-done.2, f32[6144]{0:T(1024)S(1)} %sqrt.28), kind=kOutput, calls=%fused_computation.7 | convolution fusion | flops 176332800 | bytes 7032832 | tf_op jit(solution)/shard_map/dot_general | solution.py:18
  36.4 4.4 %reshape.57 = f32[256,24,28]{1,0,2:T(8,128)} reshape(f32[6144,28]{0,1:T(8,128)S(1)} %convolution_multiply_fusion) | data formatting | bytes 1376256 | tf_op jit(solution)/shard_map/reshape | solution.py:41
  40.8 3.1 %fusion.17 = (f32[24,28]{0,1:T(8,128)S(1)}, f32[256,28]{0,1:T(8,128)S(1)}) fusion(f32[256,24,28]{1,0,2:T(8,128)} %reshape.57), kind=kLoop, calls=%fused_computation.42 | loop fusion | flops 336224 | bytes 719488 | tf_op jit(solution)/shard_map/reduce_sum | solution.py:43
  43.9 0.1 copy.15
  44.0 65.5 %all-reduce.1 = (f32[24,28]{1,0:T(8,128)S(1)}, f32[24,512]{1,0:T(8,128)S(1)}) all-reduce(f32[24,28]{1,0:T(8,128)S(1)} %copy.15, f32[24,512]{1,0:T(8,128)S(1)} %get-tuple-element.12), channel_id=1, replica_groups=mesh['store'=16,'dept'=16] {'store'}, use_global_device_ids=true, to_apply=%region_10.11 | all-reduce | flops 12960 | bytes 103680 | tf_op jit(solution)/shard_map/psum | solution.py:45
  109.5 0.1 multiply_reduce_fusion.2
  109.6 2.2 copy.14
  111.8 2.4 %reshape.56 = f32[256,672]{1,0:T(8,128)S(1)} reshape(f32[6144,28]{1,0:T(8,128)} %copy.14) | data formatting | bytes 1376256 | tf_op jit(solution)/shard_map/reshape | solution.py:41
  114.3 0.4 fusion.5
  114.6 0.2 fusion.18
  114.8 53.4 %all-reduce = (f32[256,28]{0,1:T(8,128)S(1)}, f32[28]{0:T(128)S(1)}) all-reduce(f32[256,28]{0,1:T(8,128)S(1)} %get-tuple-element.16, f32[28]{0:T(128)S(1)} %get-tuple-element.27), channel_id=1, replica_groups=mesh['store'=16,'dept'=16] {'dept'}, use_global_device_ids=true, to_apply=%region_5.6 | all-reduce | flops 7196 | bytes 57568 | tf_op jit(solution)/shard_map/psum | solution.py:44
  168.2 1.2 multiply_reduce_fusion.1
  169.4 1.6 fusion.3
  171.0 0.3 fusion.19
  171.3 50.7 %psum.47 = f32[28]{0:T(128)S(1)} all-reduce(f32[28]{0:T(128)S(1)} %get-tuple-element.29), channel_id=1, replica_groups=mesh['store'=16,'dept'=16] {'store'}, use_global_device_ids=true, to_apply=%region_14.15 | all-reduce | flops 28 | bytes 224 | tf_op jit(solution)/shard_map/psum | solution.py:48
  222.0 0.6 multiply_bitcast_fusion.1
  222.6 0.1 add.73
  222.7 0.6 multiply_bitcast_fusion
  223.3 0.1 add.70
  223.4 0.1 add.71
  223.5 0.3 copy.16
  223.8 0.1 add_add_fusion
  223.9 1.1 copy.17
  (8 shorter events, 0.1 us)
Async XLA Ops:
  7.2 14.1 %copy-start = (bf16[512,512]{1,0:T(8,128)(2,1)S(1)}, bf16[512,512]{1,0:T(8,128)(2,1)}, u32[]{:S(2)}) copy-start(bf16[512,512]{1,0:T(8,128)(2,1)} %param.6) | copy-start | bytes 1572868
  7.2 161.0 %all-reduce.4.cloned.1.call-start = ((), (), s32[]{:S(2)}) async-start(), calls=%async_computation | async-start | bytes 1048576 | tf_op jit(solution)/shard_map/psum | solution.py:28
  14.0 7.3 %copy-start.1 = (bf16[512,512]{1,0:T(8,128)(2,1)S(1)}, bf16[512,512]{1,0:T(8,128)(2,1)}, u32[]{:S(2)}) copy-start(bf16[512,512]{1,0:T(8,128)(2,1)} %param.5) | copy-start | bytes 1572868
  21.3 10.4 %copy-start.2 = (bf16[512,28]{0,1:T(8,128)(2,1)S(1)}, bf16[512,28]{0,1:T(8,128)(2,1)}, u32[]{:S(2)}) copy-start(bf16[512,28]{0,1:T(8,128)(2,1)} %param.7) | copy-start | bytes 86020
Sparse Core Ops, SparseCore 0:
  14.0 130.8 all-reduce.3
where the time goes:
time: 232 us
  blocking collectives  170 us (73%)
  other arithmetic  19.6 us (8%)
  matrix products  17.5 us (8%)
  between operations  14.1 us (6%)
  local copies, waits for them, and re-layouts  10.9 us (5%)
    psum x1, blocking collectives, body(): col_sum = lax.psum(col_part, 'store')  65.5 us
    psum x1, blocking collectives, body(): row_sum = lax.psum(row_part, 'dept')  53.4 us
    psum x1, blocking collectives, body(): err_s = lax.psum(jnp.sum(store_err, axis=0), 'store')  50.7 us
    dot_general x3, matrix products, predictor_function(): jnp.dot(hidden_one, middle_layer_matrix, preferred_element_type=jnp.float32)  12.4 us
    convert_element_type x1, other arithmetic, predictor_function(): scaled = (values / root_mean).astype(jnp.bfloat16)  7.24 us
    reshape x2, local copies, waits for them, and re-layouts, body(): finest_tier = finest_tier.reshape(store_row_set, item_columns, horizon)  6.88 us
    reduce_sum x1, other arithmetic, body(): item_part = jnp.sum(widened_entries, axis=0)  6.59 us
    dot_general x3, matrix products, predictor_function(): jnp.dot(hidden_two, final_layer_matrix, preferred_element_type=jnp.float32)  5.15 us
  transfers between devices with their start and end apart: 1, of which 0 were waited for; matrix products, arithmetic and copies ran while one was open for 15% of the time, Pallas kernels for 0%

commit v1 on v0

--- a/solution.py
+++ b/solution.py
@@ -41,7 +41,8 @@
     finest_tier = finest_tier.reshape(store_row_set, item_columns, horizon)
     row_part = jnp.sum(finest_tier, axis=1)
     col_part = jnp.sum(finest_tier, axis=0)
-    row_sum = lax.psum(row_part, "dept")
+    parts = lax.all_gather(row_part, "dept")
+    row_sum = jnp.sum(parts, axis=0)
     col_sum = lax.psum(col_part, "store")
     store_err = outlet_estimate - row_sum
     item_err = product_estimate - col_sum

time: 232 us -> 266 us (1.15)
  the two profiles are of different devices: /device:TPU:1 before, /device:TPU:0 now
where the time goes in v1:
time: 266 us; the launch traced here: 265 us
  blocking collectives  137 us (52%)
  waiting for transfers between devices  65.4 us (25%)
  other arithmetic  19.8 us (7%)
  matrix products  17.6 us (7%)
  between operations  14.1 us (5%)
  local copies, waits for them, and re-layouts  11.1 us (4%)
    psum x1, waiting for transfers between devices, body(): outlet_past_sales = lax.psum(store_part, 'dept')  65.4 us
    psum x1, blocking collectives, body(): err_s = lax.psum(jnp.sum(store_err, axis=0), 'store')  65 us
    all_gather x1, blocking collectives, body(): parts = lax.all_gather(row_part, 'dept')  37.9 us
    psum x1, blocking collectives, body(): err_i = lax.psum(jnp.sum(item_err, axis=0), 'dept')  34.3 us
    dot_general x3, matrix products, predictor_function(): jnp.dot(hidden_one, middle_layer_matrix, preferred_element_type=jnp.float32)  12.4 us
    convert_element_type x1, other arithmetic, predictor_function(): scaled = (values / root_mean).astype(jnp.bfloat16)  7.36 us
    reshape x2, local copies, waits for them, and re-layouts, body(): finest_tier = finest_tier.reshape(store_row_set, item_columns, horizon)  6.86 us
    reduce_sum x1, other arithmetic, body(): item_part = jnp.sum(widened_entries, axis=0)  6.59 us
  transfers between devices with their start and end apart: 1, of which 1 were waited for; matrix products, arithmetic and copies ran while one was open for 13% of the time, Pallas kernels for 0%

profile of v1, /device:TPU:0, one launch (start us, length us, event | category | flops | bytes accessed | tf_op | source)
XLA Modules:
  0.0 265.3 jit_solution(12750152055746011380)
XLA Ops:
  7.2 0.0 all-reduce.3.cloned.1.call-start
  7.2 6.6 %convert_reduce_fusion = (f32[24,512]{1,0:T(8,128)S(1)}, f32[256,24]{1,0:T(8,128)S(1)}, f32[256,512]{1,0:T(8,128)}) fusion(bf16[256,24,512]{2,1,0:T(8,128)(2,1)} %param.4), kind=kLoop, calls=%fused_computation.5 | loop fusion | flops 15579136 | bytes 6889472 | tf_op jit(solution)/shard_map/reduce_sum | solution.py:26
  13.8 0.0 all-reduce.3.cloned.1.call-update
  13.9 0.1 sqrt.28
  14.0 7.4 %fusion = bf16[6144,512]{1,0:T(8,128)(2,1)} fusion(bf16[256,24,512]{2,1,0:T(8,128)(2,1)} %param.4, f32[6144]{0:T(1024)S(1)} %sqrt.28), kind=kLoop, calls=%fused_computation.1 | loop fusion | flops 9437184 | bytes 12607488 | tf_op jit(solution)/shard_map/convert_element_type | solution.py:11
  21.4 10.4 %maximum_convert_fusion = bf16[6144,512]{1,0:T(8,128)(2,1)} fusion(bf16[512,512]{1,0:T(8,128)(2,1)S(1)} %copy-done, bf16[6144,512]{1,0:T(8,128)(2,1)} %fusion, bf16[512,512]{1,0:T(8,128)(2,1)S(1)} %copy-done.1), kind=kOutput, calls=%fused_computation.2 | convolution fusion | flops 6455033856 | bytes 13631488 | tf_op jit(solution)/shard_map/dot_general | solution.py:16
  31.8 4.7 %convolution_multiply_fusion = f32[6144,28]{0,1:T(8,128)S(1)} fusion(bf16[6144,512]{1,0:T(8,128)(2,1)} %maximum_convert_fusion, bf16[512,28]{0,1:T(8,128)(2,1)S(1)} %copy-done.2, f32[6144]{0:T(1024)S(1)} %sqrt.28), kind=kOutput, calls=%fused_computation.7 | convolution fusion | flops 176332800 | bytes 7032832 | tf_op jit(solution)/shard_map/dot_general | solution.py:18
  36.5 2.3 copy.14
  38.8 4.4 %reshape.57 = f32[256,24,28]{1,0,2:T(8,128)} reshape(f32[6144,28]{0,1:T(8,128)S(1)} %convolution_multiply_fusion) | data formatting | bytes 1376256 | tf_op jit(solution)/shard_map/reshape | solution.py:41
  43.3 2.4 reshape.56
  45.7 3.1 %fusion.17 = (f32[24,28]{0,1:T(8,128)S(1)}, f32[256,28]{0,1:T(8,128)S(1)}) fusion(f32[256,24,28]{1,0,2:T(8,128)} %reshape.57), kind=kLoop, calls=%fused_computation.43 | loop fusion | flops 336224 | bytes 719488 | tf_op jit(solution)/shard_map/reduce_sum | solution.py:43
  48.8 0.1 copy.15
  48.8 37.9 %all-gather = f32[4096,28]{0,1:T(8,128)S(1)} all-gather(f32[256,28]{0,1:T(8,128)S(1)} %get-tuple-element.16), channel_id=2, replica_groups=mesh['store'=16,'dept'=16] {'dept'}, dimensions={0}, use_global_device_ids=true | all-gather | bytes 487424 | tf_op jit(solution)/shard_map/all_gather | solution.py:44
  86.8 0.2 copy.18
  86.9 0.1 bitcast_reduce_fusion
  87.0 65.4 %all-reduce.3.cloned.1.call-done = f32[256,512]{1,0:T(8,128)} async-done(((f32[256,512]{1,0:T(8,128)}), f32[256,512]{1,0:T(8,128)}) %all-reduce.3.cloned.1.call-update) | async-done | bytes 524304 | tf_op jit(solution)/shard_map/psum | solution.py:28
  152.5 1.2 multiply_reduce_fusion.1
  153.6 1.6 fusion.3
  155.2 0.3 fusion.18
  155.5 65.0 %all-reduce = (f32[28]{0:T(128)S(1)}, f32[24,28]{1,0:T(8,128)S(1)}, f32[24,512]{1,0:T(8,128)S(1)}) all-reduce(f32[28]{0:T(128)S(1)} %get-tuple-element.26, f32[24,28]{1,0:T(8,128)S(1)} %copy.15, f32[24,512]{1,0:T(8,128)S(1)} %get-tuple-element.12), channel_id=1, replica_groups=mesh['store'=16,'dept'=16] {'store'}, use_global_device_ids=true, to_apply=%region_14.15 | all-reduce | flops 12988 | bytes 103904 | tf_op jit(solution)/shard_map/psum | solution.py:49
  220.6 0.1 multiply_reduce_fusion.2
  220.7 0.4 fusion.5
  221.1 0.2 fusion.19
  221.2 34.3 %psum.38 = f32[28]{0:T(128)S(1)} all-reduce(f32[28]{0:T(128)S(1)} %get-tuple-element.28), channel_id=1, replica_groups=mesh['store'=16,'dept'=16] {'dept'}, use_global_device_ids=true, to_apply=%region_12.13 | all-reduce | flops 28 | bytes 224 | tf_op jit(solution)/shard_map/psum | solution.py:50
  255.5 0.6 multiply_bitcast_fusion.1
  256.1 0.1 add.71
  256.2 0.6 multiply_bitcast_fusion
  256.8 0.1 add.68
  256.9 0.1 add.69
  257.0 0.3 copy.16
  257.3 0.1 add_add_fusion
  257.4 1.1 copy.17
  (10 shorter events, 0.1 us)
Async XLA Ops:
  7.2 14.2 %copy-start = (bf16[512,512]{1,0:T(8,128)(2,1)S(1)}, bf16[512,512]{1,0:T(8,128)(2,1)}, u32[]{:S(2)}) copy-start(bf16[512,512]{1,0:T(8,128)(2,1)} %param.6) | copy-start | bytes 1572868
  7.2 145.3 %all-reduce.3.cloned.1.call-start = ((), (), s32[]{:S(2)}) async-start(), calls=%async_computation | async-start | bytes 1048576 | tf_op jit(solution)/shard_map/psum | solution.py:28
  14.0 7.4 %copy-start.1 = (bf16[512,512]{1,0:T(8,128)(2,1)S(1)}, bf16[512,512]{1,0:T(8,128)(2,1)}, u32[]{:S(2)}) copy-start(bf16[512,512]{1,0:T(8,128)(2,1)} %param.5) | copy-start | bytes 1572868
  21.4 10.4 %copy-start.2 = (bf16[512,28]{0,1:T(8,128)(2,1)S(1)}, bf16[512,28]{0,1:T(8,128)(2,1)}, u32[]{:S(2)}) copy-start(bf16[512,28]{0,1:T(8,128)(2,1)} %param.7) | copy-start | bytes 86020
Sparse Core Ops, SparseCore 0:
  14.0 138.4 all-reduce.2
